TPU v7x, 128 devices: a whole 4x4x4 slice. The times are simulated.
128 devices in a mesh: outer: 8 (over z, core), inner: 16 (over y, x).
Axes of the slice: x: 4, y: 4, z: 4, core: 2. Of those that a mesh axis runs over, the one named last changes fastest.
Arguments:
- tokens_in: bfloat16 [16384, 2048], P(('outer', 'inner')), may hold values from -6 to 6
- expert_ids: int32 [16384, 10], P(('outer', 'inner')), may hold values from 0 to 255, all different within a row; in each aligned block of 128 rows (0 to 127, 128 to 255, ...) at most 6 rows name the same one
- route_weight: float32 [16384, 10], P(('outer', 'inner')), may hold values from 0.05 to 1
- first_gain: float32 [2048], replicated, may hold values from 0.5 to 1.5
- gate_weight: bfloat16 [256, 2048, 512], P(('outer', 'inner')), may hold values from -0.125 to 0.125
- up_weight: bfloat16 [256, 2048, 512], P(('outer', 'inner')), may hold values from -0.125 to 0.125
- down_weight: bfloat16 [256, 512, 2048], P(('outer', 'inner')), may hold values from -0.25 to 0.25
- second_gain: float32 [2048], replicated, may hold values from 0.5 to 1.5
- mixer_weight: bfloat16 [2048, 4096], P(None, 'inner'), may hold values from -0.125 to 0.125
- gating_weight: bfloat16 [2048, 32], replicated, may hold values from -0.125 to 0.125
- filter_taps: bfloat16 [4, 4096], replicated, may hold values from -3 to 3
- decay_log: float32 [16], replicated, may hold values from -9 to -3
- decay_bias: float32 [16], replicated, may hold values from -1 to 1
- output_gain: float32 [128], replicated, may hold values from 0.5 to 1.5
Outputs:
- hidden_out: bfloat16 [16384, 2048], P(('outer', 'inner'))
- core_out: bfloat16 [16384, 2048], P(('outer', 'inner'))
Inputs may be any that keep to these rules, and one draw needn't show every extreme that they name: `expert_ids`: each token names 10 different experts; the 128 rows of one device name any one expert at most 6 times, a bound that some block reaches.
All inputs are finite; a program needn't handle non-finite values.
Results may differ from a plain program's by a relative error of at most 0.015.
Values may be sent and summed in bfloat16 or wider, within the bound.
A program may use at most 576 MiB of HBM per device.

v0:
```python
import jax
import jax.numpy as jnp
from jax import lax
from jax.sharding import PartitionSpec as P


def shifted(value, axis, steps):
    count = lax.axis_size(axis)
    leading, last = (max(0, -steps), min(count, count - steps))
    return lax.ppermute(value, axis, [(source, source + steps) for source in range(leading, last)])


def prefix_2(x, axis, join, neutral):
    place = lax.axis_index(axis)
    gathered = jax.tree.map(
        lambda a, kind: lax.all_gather(a.astype(kind), axis), x, (jnp.bfloat16, jnp.bfloat16)
    )
    state = jax.tree.map(lambda a, e: jnp.zeros_like(a) + jnp.asarray(e, a.dtype), x, neutral)

    def one(lap, state):
        return join(
            state,
            jax.tree.map(
                lambda a, own: lax.dynamic_index_in_dim(a, lap, 0, False).astype(own.dtype),
                gathered,
                x,
            ),
        )

    return lax.fori_loop(0, place, one, state)


def shortened(x):

    def short(part):
        return part.astype(jnp.bfloat16) if part.dtype == jnp.float32 else part

    return jax.tree.map(short, x)


def spread_2(value, axis, source):
    kept = jnp.where(lax.axis_index(axis) == source, value, 0).astype(value.dtype)
    return lax.psum(kept, axis)


def entering(x, axis, combine, identity):
    length, place = (lax.axis_size(axis), lax.axis_index(axis))
    everything = jax.tree.map(
        lambda part, kind: lax.all_gather(part.astype(kind), axis),
        x,
        jax.tree.map(lambda a: jnp.bfloat16 if a.dtype == jnp.float32 else a.dtype, x),
    )
    start = jax.tree.map(
        lambda part, zero: jnp.broadcast_to(jnp.asarray(zero, part.dtype), part.shape), x, identity
    )

    def lap(k, before):
        reached = k < place
        new = combine(
            before, jax.tree.map(lambda part, own: part[k].astype(own.dtype), everything, x)
        )
        return jax.tree.map(lambda a, b: jnp.where(reached, a, b), new, before)

    return lax.fori_loop(0, length, lap, start)


def rms_scale(values, gain):
    wide = values.astype(jnp.float32)
    return wide * lax.rsqrt(jnp.mean(wide * wide, axis=-1, keepdims=True) + 1e-06) * gain


def unit_heads(values):
    return values * lax.rsqrt(jnp.sum(values * values, axis=-1, keepdims=True) + 1e-06)


def run_experts(piece, gate_weight, up_weight, down_weight):
    gate = jnp.einsum("secd,edf->secf", piece, gate_weight, preferred_element_type=jnp.float32)
    upper = jnp.einsum("secd,edf->secf", piece, up_weight, preferred_element_type=jnp.float32)
    hidden = (jax.nn.silu(gate) * upper).astype(jnp.bfloat16)
    return jnp.einsum(
        "secf,efd->secd", hidden, down_weight, preferred_element_type=jnp.float32
    ).astype(jnp.bfloat16)


def join_maps(earlier, later):
    first_map, first_state = earlier
    next_map, next_state = later
    joined_map = jnp.einsum("hij,hjk->hik", next_map, first_map, precision=lax.Precision.HIGHEST)
    joined_state = (
        jnp.einsum("hij,hjv->hiv", next_map, first_state, precision=lax.Precision.HIGHEST)
        + next_state
    )
    return (joined_map, joined_state)


def per_device(
    tokens_in,
    expert_ids,
    route_weight,
    first_gain,
    gate_weight,
    up_weight,
    down_weight,
    second_gain,
    mixer_weight,
    gating_weight,
    filter_taps,
    decay_log,
    decay_bias,
    output_gain,
):
    n_outer = lax.axis_size("outer")
    n_inner = lax.axis_size("inner")
    n_dev = n_outer * n_inner
    tok_count, width = tokens_in.shape
    top_count = expert_ids.shape[1]
    local_experts = gate_weight.shape[0]
    experts_all = local_experts * n_dev
    capacity = max(2, 6 * tok_count * top_count // (5 * experts_all))
    normed_first = rms_scale(tokens_in, first_gain).astype(jnp.bfloat16)
    mix_weight = route_weight / jnp.sum(route_weight, axis=1, keepdims=True)
    pairs = tok_count * top_count
    flat = expert_ids.reshape(-1)
    onehot = (flat[:, None] == jnp.arange(experts_all, dtype=jnp.int32)[None, :]).astype(jnp.int32)
    before = jnp.cumsum(onehot, axis=0) - onehot
    slot_index = jnp.sum(before * onehot, axis=1)
    target = (
        flat // local_experts * (local_experts * capacity)
        + flat % local_experts * capacity
        + slot_index
    )
    owner = jnp.arange(pairs, dtype=jnp.int32) // top_count
    outgoing = (
        jnp.zeros((n_dev * local_experts * capacity, width), jnp.bfloat16)
        .at[target]
        .set(normed_first[owner])
    )
    outgoing = outgoing.reshape(n_dev, local_experts, capacity, width)
    served = run_experts(
        lax.all_to_all(outgoing, ("outer", "inner"), split_axis=0, concat_axis=0, tiled=True),
        gate_weight,
        up_weight,
        down_weight,
    )
    returned = lax.all_to_all(served, ("outer", "inner"), split_axis=0, concat_axis=0, tiled=True)
    rows_back = (
        returned.reshape(-1, width)[target].astype(jnp.float32) * mix_weight.reshape(-1)[:, None]
    )
    mixture = jnp.sum(rows_back.reshape(tok_count, top_count, width), axis=1)
    hidden_out = (tokens_in.astype(jnp.float32) + mixture).astype(jnp.bfloat16)
    normed_second = rms_scale(hidden_out, second_gain).astype(jnp.bfloat16)
    mixed = jnp.dot(
        normed_second,
        lax.all_gather(mixer_weight, "inner", axis=1, tiled=True),
        preferred_element_type=jnp.float32,
    )
    projected = mixed.astype(jnp.bfloat16)
    gating = jnp.dot(normed_second, gating_weight, preferred_element_type=jnp.float32)
    taps = filter_taps.shape[0]
    rim = shifted(projected[tok_count - (taps - 1) :], ("outer", "inner"), 1)
    padded = jnp.concatenate([rim, projected], axis=0).astype(jnp.float32)
    filtered = jnp.zeros(projected.shape, jnp.float32)
    for tap_index in range(taps):
        filtered = (
            filtered
            + filter_taps[tap_index].astype(jnp.float32) * padded[tap_index : tap_index + tok_count]
        )
    filtered = jax.nn.silu(filtered)
    head_dim = output_gain.shape[0]
    value_heads = decay_log.shape[0]
    key_heads = (projected.shape[1] - value_heads * head_dim) // (2 * head_dim)
    ratio = value_heads // key_heads
    queries = unit_heads(
        filtered[:, : key_heads * head_dim].reshape(tok_count, key_heads, head_dim)
    ) * head_dim ** (-0.5)
    keys = unit_heads(
        filtered[:, key_heads * head_dim : 2 * key_heads * head_dim].reshape(
            tok_count, key_heads, head_dim
        )
    )
    values = filtered[:, 2 * key_heads * head_dim :].reshape(tok_count, value_heads, head_dim)
    queries = jnp.repeat(queries, ratio, axis=1)
    keys = jnp.repeat(keys, ratio, axis=1)
    strength = jax.nn.sigmoid(gating[:, :value_heads]).T
    log_decay = (-jnp.exp(decay_log) * jax.nn.softplus(gating[:, value_heads:] + decay_bias)).T
    cumulative = jnp.cumsum(log_decay, axis=1)
    positions = jnp.arange(tok_count)
    lower_incl = positions[:, None] >= positions[None, :]
    lower_strict = positions[:, None] > positions[None, :]
    spread = cumulative[:, :, None] - cumulative[:, None, :]
    decay_mat = jnp.where(lower_incl, jnp.exp(jnp.where(lower_incl, spread, 0.0)), 0.0)
    key_major = keys.transpose(1, 0, 2)
    query_leading = queries.transpose(1, 0, 2)
    value_major = values.transpose(1, 0, 2)
    key_inner = jnp.einsum("htd,hid->hti", key_major, key_major, precision=lax.Precision.HIGHEST)
    lower_part = jnp.where(lower_strict, decay_mat * key_inner, 0.0) * strength[:, :, None]
    system = lower_part + jnp.eye(tok_count, dtype=jnp.float32)
    growth = jnp.exp(cumulative)
    scaled_keys = key_major * (strength * growth)[:, :, None]
    scaled_values = value_major * strength[:, :, None]
    key_resolved = lax.linalg.triangular_solve(
        system, scaled_keys, left_side=True, lower=True, unit_diagonal=True
    )
    value_resolved = lax.linalg.triangular_solve(
        system, scaled_values, left_side=True, lower=True, unit_diagonal=True
    )
    tail = jnp.exp(cumulative[:, -1:] - cumulative)
    trailing_keys = key_major * tail[:, :, None]
    eye_heads = jnp.broadcast_to(
        jnp.eye(head_dim, dtype=jnp.float32), (value_heads, head_dim, head_dim)
    )
    state_map = growth[:, -1][:, None, None] * eye_heads - jnp.einsum(
        "htk,htj->hkj", trailing_keys, key_resolved, precision=lax.Precision.HIGHEST
    )
    state_increment = jnp.einsum(
        "xbe,xbz->xez", trailing_keys, value_resolved, precision=lax.Precision.HIGHEST
    )
    identity = (eye_heads, jnp.zeros_like(state_increment))
    inner_pre = prefix_2((state_map, state_increment), "inner", join_maps, identity)
    inclusive = join_maps(inner_pre, (state_map, state_increment))
    group = spread_2(shortened(jnp.stack(inclusive)), "inner", n_inner - 1)
    outer_pre = entering((group[0], group[1]), "outer", join_maps, identity)
    prefix = join_maps(outer_pre, inner_pre)
    initial_state = prefix[1]
    updates = value_resolved - jnp.einsum(
        "mwx,mxd->mwd", key_resolved, initial_state, precision=lax.Precision.HIGHEST
    )
    query_key = (
        jnp.einsum("htd,hid->hti", query_leading, key_major, precision=lax.Precision.HIGHEST)
        * decay_mat
    )
    carried = (
        jnp.einsum("mwx,mxd->mwd", query_leading, initial_state, precision=lax.Precision.HIGHEST)
        * growth[:, :, None]
    )
    attended = carried + jnp.einsum(
        "hti,hiv->htv", query_key, updates, precision=lax.Precision.HIGHEST
    )
    attended = attended.transpose(1, 0, 2)
    core_out = (
        rms_scale(attended, output_gain)
        .astype(jnp.bfloat16)
        .reshape(tok_count, value_heads * head_dim)
    )
    return (hidden_out, core_out)


def solution(mesh):
    return jax.shard_map(
        per_device,
        mesh=mesh,
        in_specs=(
            P(("outer", "inner"), None),
            P(("outer", "inner"), None),
            P(("outer", "inner"), None),
            P(),
            P(("outer", "inner"), None, None),
            P(("outer", "inner"), None, None),
            P(("outer", "inner"), None, None),
            P(),
            P(None, "inner"),
            P(),
            P(),
            P(),
            P(),
            P(),
        ),
        out_specs=(P(("outer", "inner"), None), P(("outer", "inner"), None)),
        check_vma=False,
    )
```

profile of v0, /device:TPU:1, one launch (start us, length us, event | category | flops | bytes accessed | tf_op | source)
XLA Modules:
  0.0 936.2 jit_solution(5289336182392275664)
XLA Ops:
  11.7 34.4 %scatter_custom_fusion = bf16[1536,2048]{1,0:T(8,128)(2,1)} fusion(s32[1280]{0:T(1024)S(1)} %fusion.80, bf16[128,2048]{1,0:T(8,128)(2,1)S(1)} %fusion.61, s32[2048]{0:T(1024)S(1)} %pad_clamp_fusion.1, bf16[]{:T(256)} %constant.104.clone.1), kind=kCustom, calls=%fused_computation.26 | custom fusion | bytes 6291458 | tf_op jit(solution)/shard_map/scatter | solution.py:136
  46.1 11.0 %reshape.311 = bf16[128,2,6,2048]{3,2,1,0:T(8,128)(2,1)} reshape(bf16[1536,2048]{1,0:T(8,128)(2,1)} %scatter_custom_fusion) | data formatting | bytes 12582912 | tf_op jit(solution)/shard_map/reshape | solution.py:138
  57.1 9.6 %copy.75 = bf16[128,2,6,2048]{3,1,2,0:T(2,128)(2,1)S(1)} copy(bf16[128,2,6,2048]{3,2,1,0:T(8,128)(2,1)} %reshape.311) | data formatting | bytes 12582912 | tf_op jit(solution)/shard_map/reshape | solution.py:138
  66.7 110.7 %all_to_all.10 = bf16[128,2,6,2048]{3,1,2,0:T(2,128)(2,1)S(1)} all-to-all(bf16[128,2,6,2048]{3,1,2,0:T(2,128)(2,1)S(1)} %copy.75), channel_id=1, replica_groups=mesh['outer'=8,'inner'=16] {'outer','inner'}, dimensions={0} | all-to-all | bytes 12582912 | tf_op jit(solution)/shard_map/all_to_all | solution.py:140
  177.5 2.6 copy-done.8
  180.1 8.6 fusion.15
  188.7 19.6 %convert_bitcast_fusion = bf16[128,2,6,2048]{3,0,2,1:T(8,128)(2,1)} fusion(bf16[2,512,2048]{2,1,0:T(8,128)(2,1)} %param.26, f32[2,128,6,512]{3,1,2,0:T(8,128)} %fusion.15, bf16[2,2048,512]{2,1,0:T(8,128)(2,1)} %param.24, bf16[128,2,6,2048]{3,1,2,0:T(2,128)(2,1)} %copy-done.8), kind=kOutput, calls=%fused_computation.21 | convolution fusion | flops 6450315264 | bytes 24117248 | tf_op jit(solution)/shard_map/secf,efd->secd/dot_general | solution.py:80
  208.4 12.8 %copy.78 = bf16[128,2,6,2048]{3,1,2,0:T(2,128)(2,1)} copy(bf16[128,2,6,2048]{3,0,2,1:T(8,128)(2,1)} %convert_bitcast_fusion) | data formatting | bytes 12582912 | tf_op jit(solution)/shard_map/convert_element_type | solution.py:82
  221.1 7.9 all-to-all-start.1
  229.5 74.2 %all-to-all-done.1 = bf16[128,2,6,2048]{3,1,2,0:T(2,128)(2,1)} async-done(((bf16[128,2,6,2048]{3,1,2,0:T(2,128)(2,1)}), bf16[128,2,6,2048]{3,1,2,0:T(2,128)(2,1)}, u32[]{:S(2)}, u32[]{:S(2)}) %all-to-all-start.1) | async-done | bytes 6291488 | tf_op jit(solution)/shard_map/all_to_all | solution.py:145
  303.7 10.4 %copy.79 = bf16[128,2,6,2048]{3,2,1,0:T(8,128)(2,1)} copy(bf16[128,2,6,2048]{3,1,2,0:T(2,128)(2,1)} %all-to-all-done.1) | data formatting | bytes 12582912 | tf_op jit(solution)/shard_map/all_to_all | solution.py:145
  314.1 11.4 %reshape.312 = bf16[1536,2048]{1,0:T(8,128)(2,1)} reshape(bf16[128,2,6,2048]{3,2,1,0:T(8,128)(2,1)} %copy.79) | data formatting | bytes 12582912 | tf_op jit(solution)/shard_map/reshape | solution.py:147
  325.5 14.4 %gather_fusion = bf16[1280,2048]{1,0:T(8,128)(2,1)} fusion(bf16[1536,2048]{1,0:T(8,128)(2,1)} %reshape.312, s32[2048]{0:T(1024)S(1)} %pad_clamp_fusion), kind=kCustom, calls=%fused_computation.1 | custom fusion | bytes 10490880 | tf_op jit(solution)/shard_map/gather | solution.py:147
  339.9 10.3 %reshape.322 = f32[128,10,2048]{2,1,0:T(8,128)} reshape(bf16[1280,2048]{1,0:T(8,128)(2,1)} %gather_fusion) | data formatting | bytes 15728640 | tf_op jit(solution)/shard_map/convert_element_type | solution.py:147
  350.3 9.5 %multiply_reduce_fusion = f32[128,2048]{1,0:T(8,128)S(1)} fusion(f32[128,10,2048]{2,1,0:T(8,128)} %reshape.322, f32[128,10]{1,0:T(8,128)S(1)} %copy.80), kind=kLoop, calls=%fused_computation.20 | loop fusion | flops 4980736 | bytes 11539456 | tf_op jit(solution)/shard_map/reduce_sum | solution.py:149
  361.0 8.2 convolution_convert_fusion
  369.3 4.0 collective-permute-start
  373.4 4.5 collective-permute-done
  382.2 3.4 fusion.50
  385.6 157.9 %custom-call.5 = f32[16,1,128,128]{2,3,1,0:T(8,128)S(1)} custom-call(f32[16,1,128,128]{3,2,1,0:T(8,128)} %fusion.50), custom_call_target="InvertDiagBlocksLowerTriangular" | custom-call | tf_op jit(solution)/shard_map/triangular_solve/custom-call.1 | solution.py:201
  550.3 3.0 fusion.89
  553.8 3.1 fusion.65
  556.9 2.8 fusion.88
  559.7 60.0 %all-gather.16.cloned.1.call-done = bf16[256,128,128]{2,1,0:T(8,128)(2,1)} async-done(((bf16[16,128,128]{2,1,0:T(8,128)(2,1)}), bf16[256,128,128]{2,1,0:T(8,128)(2,1)}) %all-gather.16.cloned.1.call-update) | async-done | bytes 8388624 | tf_op jit(solution)/shard_map/all_gather | solution.py:16
  619.7 72.5 %all-gather.14.cloned.1.call-done = bf16[256,128,128]{2,1,0:T(8,128)(2,1)} async-done(((bf16[16,128,128]{2,1,0:T(8,128)(2,1)}), bf16[256,128,128]{2,1,0:T(8,128)(2,1)}) %all-gather.14.cloned.1.call-update) | async-done | bytes 8388624 | tf_op jit(solution)/shard_map/all_gather | solution.py:16
  693.6 2.4 fusion.55
  697.2 141.7 %all-reduce.2.cloned.1.call-done = bf16[2,16,128,128]{3,2,1,0:T(8,128)(2,1)} async-done(((bf16[2,16,128,128]{3,2,1,0:T(8,128)(2,1)}), bf16[2,16,128,128]{3,2,1,0:T(8,128)(2,1)}) %all-reduce.2.cloned.1.call-update) | async-done | bytes 1048592 | tf_op jit(solution)/shard_map/psum | solution.py:43
  838.9 2.3 fusion.87
  843.6 3.3 convolution_multiply_fusion
  846.9 27.9 %all-gather.10.cloned.1.call-done = bf16[8,16,128,128]{3,2,1,0:T(8,128)(2,1)} async-done(((bf16[1,16,128,128]{3,2,1,0:T(8,128)(2,1)}), bf16[8,16,128,128]{3,2,1,0:T(8,128)(2,1)}) %all-gather.10.cloned.1.call-update) | async-done | bytes 4194320 | tf_op jit(solution)/shard_map/all_gather | solution.py:49
  874.8 33.7 %all-gather.12.cloned.1.call-done = bf16[8,16,128,128]{3,2,1,0:T(8,128)(2,1)} async-done(((bf16[1,16,128,128]{3,2,1,0:T(8,128)(2,1)}), bf16[8,16,128,128]{3,2,1,0:T(8,128)(2,1)}) %all-gather.12.cloned.1.call-update) | async-done | bytes 4194320 | tf_op jit(solution)/shard_map/all_gather | solution.py:49
  908.6 12.7 %while.27 = (s32[]{:T(128)}, bf16[16,128,128]{2,1,0:T(8,128)(2,1)S(1)}, s32[]{:T(128)}, bf16[8,16,128,128]{3,2,1,0:T(8,128)(2,1)}, bf16[8,16,128,128]{3,2,1,0:T(8,128)(2,1)}, /*index=5*/s32[]{:T(128)}, s32[]{:T(128)}) while((s32[]{:T(128)}, bf16[16,128,128]{2,1,0:T(8,128)(2,1)S(1)}, s32[]{:T(128)}, ...), condition=%wide.region_15.17_spmd.clone, body=%wide.region_14.16_spmd.clone.sunk | while | flops 68157440 | bytes 3672671 | solution.py:64
  (148 shorter events, 42.4 us)
Async XLA Ops:
  7.2 352.9 %copy-start = (bf16[2048,32]{0,1:T(8,128)(2,1)S(1)}, bf16[2048,32]{0,1:T(8,128)(2,1)}, u32[]{:S(2)}) copy-start(bf16[2048,32]{0,1:T(8,128)(2,1)} %param.29) | copy-start | bytes 393220
  7.2 353.8 %all-gather.8.cloned.1.call-start = ((), (), s32[]{:S(2)}) async-start(), calls=%async_computation.2 | async-start | bytes 17825792 | tf_op jit(solution)/shard_map/all_gather | solution.py:154
  9.6 1.6 copy-start.9
  9.6 1.8 copy-start.20
  66.7 113.4 %copy-start.23 = (bf16[2,2048,512]{2,1,0:T(8,128)(2,1)S(1)}, bf16[2,2048,512]{2,1,0:T(8,128)(2,1)}, u32[]{:S(2)}) copy-start(bf16[2,2048,512]{2,1,0:T(8,128)(2,1)} %param.25) | copy-start | bytes 12582916
  177.5 2.6 copy-start.8
  221.1 8.0 copy-start.19
  221.1 8.2 copy-start.24
  221.1 8.4 copy-start.17
  221.1 82.6 %all-to-all-start.1 = ((bf16[128,2,6,2048]{3,1,2,0:T(2,128)(2,1)}), bf16[128,2,6,2048]{3,1,2,0:T(2,128)(2,1)}, u32[]{:S(2)}, u32[]{:S(2)}) async-start(bf16[128,2,6,2048]{3,1,2,0:T(2,128)(2,1)} %copy.78), calls=%async_computation.1 | async-start | bytes 12582912 | tf_op jit(solution)/shard_map/all_to_all | solution.py:145
  229.1 390.6 %all-gather.16.cloned.1.call-start = ((), (), s32[]{:S(2)}) async-start(), calls=%async_computation.7 | async-start | bytes 8912896 | tf_op jit(solution)/shard_map/all_gather | solution.py:16
  350.3 9.8 %copy-start.18 = (f32[2048]{0:T(1024)S(1)}, f32[2048]{0:T(1024)}, u32[]{:S(2)}) copy-start(f32[2048]{0:T(1024)} %param.27) | copy-start | bytes 24580
  350.3 10.2 %copy-start.21 = (f32[16]{0:T(128)S(1)}, f32[16]{0:T(128)}, u32[]{:S(2)}) copy-start(f32[16]{0:T(128)} %param.32) | copy-start | bytes 196
  360.0 9.2 copy-start.15
  369.3 8.6 collective-permute-start
  379.5 1.7 copy-start.7
  381.2 162.4 %slice-start = ((f32[128,4096]{1,0:T(8,128)}), f32[128,2048]{1,0:T(8,128)S(1)}, s32[]{:S(2)}) async-start(f32[128,4096]{1,0:T(8,128)} %copy-done.7), calls=%async_computation.8 | async-start | bytes 2097152 | tf_op jit(solution)/shard_map/slice | solution.py:181
  543.6 6.7 copy-start.10
  548.6 1.7 copy-start.3
  550.3 3.5 copy-start.11
  553.4 138.8 %all-gather.14.cloned.1.call-start = ((), (), s32[]{:S(2)}) async-start(), calls=%async_computation.6 | async-start | bytes 8912896 | tf_op jit(solution)/shard_map/all_gather | solution.py:16
  556.9 135.3 %copy-start.5 = (f32[16,128,128]{2,1,0:T(8,128)}, f32[16,128,128]{2,1,0:T(8,128)S(1)}, u32[]{:S(2)}) copy-start(f32[16,128,128]{2,1,0:T(8,128)S(1)} %fusion.65) | copy-start | bytes 3145732
  559.6 279.2 %all-reduce.2.cloned.1.call-start = ((), (), s32[]{:S(2)}) async-start(), calls=%async_computation.3 | async-start | bytes 2097152 | tf_op jit(solution)/shard_map/psum | solution.py:43
  696.0 145.8 %copy-start.16 = (f32[16,8,8,128]{3,1,2,0:T(8,128)S(1)}, f32[16,8,8,128]{3,1,2,0:T(8,128)}, u32[]{:S(2)}) copy-start(f32[16,8,8,128]{3,1,2,0:T(8,128)} %get-tuple-element.185) | copy-start | bytes 1572868
  697.1 177.7 %all-gather.10.cloned.1.call-start = ((), (), s32[]{:S(2)}) async-start(), calls=%async_computation.4 | async-start | bytes 4718592 | tf_op jit(solution)/shard_map/all_gather | solution.py:49
  841.2 67.4 %all-gather.12.cloned.1.call-start = ((), (), s32[]{:S(2)}) async-start(), calls=%async_computation.5 | async-start | bytes 4718592 | tf_op jit(solution)/shard_map/all_gather | solution.py:49
  841.8 1.8 copy-start.13
  921.2 1.2 copy-start.4
  921.2 1.5 copy-start.6
  921.2 2.7 copy-start.2
  922.8 3.1 copy-start.14
  924.0 3.9 copy-start.22
  (2 other events, 2.0 us)
Sparse Core Ops, SparseCore 0:
  10.1 187.0 all-gather.7
  553.5 66.1 all-gather.15
  621.8 70.3 all-gather.13
  697.2 141.5 all-reduce.1
  841.3 33.4 all-gather.9
  876.4 32.1 all-gather.11
where the time goes:
time: 942 us; the launch traced here: 936 us
  waiting for transfers between devices  416 us (44%)
  other arithmetic  175 us (19%)
  local copies, waits for them, and re-layouts  131 us (14%)
  blocking collectives  111 us (12%)
  matrix products  75.8 us (8%)
  between operations  15.1 us (2%)
  starting transfers between devices  12.7 us (1%)
    another operation x4, other arithmetic, per_device(): lax.linalg.triangular_solve(system, scaled_keys, left_side=True, lower=Tr...  158 us
    psum x1, waiting for transfers between devices, spread_2(): return lax.psum(kept, axis)  142 us
    all_gather x2, waiting for transfers between devices, prefix_2(): lax.all_gather(a.astype(kind), axis)  132 us
    all_to_all x1, blocking collectives, per_device(): lax.all_to_all(outgoing, ('outer', 'inner'), split_axis=0, concat_axis=0,...  111 us
    all_to_all x1, waiting for transfers between devices, per_device(): lax.all_to_all(served, ('outer', 'inner'), split_axis=0, concat_axis=0, t...  74.2 us
    all_gather x2, waiting for transfers between devices, entering(): lax.all_gather(part.astype(kind), axis)  61.6 us
    scatter x1, local copies, waits for them, and re-layouts, per_device(): outgoing = jnp.zeros((n_dev * local_experts * capacity, width), jnp.bfloa...  34.4 us
    reshape x2, local copies, waits for them, and re-layouts, per_device(): outgoing = outgoing.reshape(n_dev, local_experts, capacity, width)  20.6 us
  transfers between devices with their start and end apart: 8, of which 7 were waited for; matrix products, arithmetic and copies ran while one was open for 18% of the time, Pallas kernels for 0%

commit v1 on v0

--- a/solution.py
+++ b/solution.py
@@ -2,6 +2,7 @@
 import jax.numpy as jnp
 from jax import lax
 from jax.sharding import PartitionSpec as P
+from jax.lax import all_gather
 
 
 def shifted(value, axis, steps):
@@ -40,7 +41,8 @@
 
 def spread_2(value, axis, source):
     kept = jnp.where(lax.axis_index(axis) == source, value, 0).astype(value.dtype)
-    return lax.psum(kept, axis)
+    matrix_use = lambda sheet, dev_axis: jnp.sum(all_gather(sheet, axis_name=dev_axis), axis=0)
+    return matrix_use(kept, axis)
 
 
 def entering(x, axis, combine, identity):

time: 942 us -> 975 us (1.035)
  waiting for transfers between devices: 416 us -> 439 us
  other arithmetic: 175 us -> 185 us
    all_gather x0 -> x1, waiting for transfers between devices: none -> 167 us  [spread_2(): all_gather(sheet, axis_name=dev_axis)]
    psum x1 -> x0, waiting for transfers between devices: 142 us -> none  [spread_2(): return lax.psum(kept, axis)]
  transfers between devices with their start and end apart: 8 -> 8, of which waited for: 7 -> 7; matrix products, arithmetic and copies ran while one was open for 18% -> 17% of each run, Pallas kernels for 0% -> 0%
where the time goes in v1:
time: 975 us; the launch traced here: 969 us
  waiting for transfers between devices  439 us (45%)
  other arithmetic  185 us (19%)
  local copies, waits for them, and re-layouts  131 us (13%)
  blocking collectives  111 us (11%)
  matrix products  75.8 us (8%)
  between operations  15.1 us (2%)
  starting transfers between devices  12.7 us (1%)
    all_gather x1, waiting for transfers between devices, spread_2(): all_gather(sheet, axis_name=dev_axis)  167 us
    another operation x4, other arithmetic, per_device(): lax.linalg.triangular_solve(system, scaled_keys, left_side=True, lower=Tr...  158 us
    all_gather x2, waiting for transfers between devices, prefix_2(): lax.all_gather(a.astype(kind), axis)  132 us
    all_to_all x1, blocking collectives, per_device(): lax.all_to_all(outgoing, ('outer', 'inner'), split_axis=0, concat_axis=0,...  111 us
    all_to_all x1, waiting for transfers between devices, per_device(): lax.all_to_all(served, ('outer', 'inner'), split_axis=0, concat_axis=0, t...  74.2 us
    all_gather x2, waiting for transfers between devices, entering(): lax.all_gather(part.astype(kind), axis)  59.5 us
    scatter x1, local copies, waits for them, and re-layouts, per_device(): outgoing = jnp.zeros((n_dev * local_experts * capacity, width), jnp.bfloa...  34.4 us
    reshape x2, local copies, waits for them, and re-layouts, per_device(): outgoing = outgoing.reshape(n_dev, local_experts, capacity, width)  20.6 us
  transfers between devices with their start and end apart: 8, of which 7 were waited for; matrix products, arithmetic and copies ran while one was open for 17% of the time, Pallas kernels for 0%

profile of v1, /device:TPU:1, one launch (start us, length us, event | category | flops | bytes accessed | tf_op | source)
XLA Modules:
  0.0 969.0 jit_solution(7619046856805840864)
XLA Ops:
  11.7 34.4 %scatter_custom_fusion = bf16[1536,2048]{1,0:T(8,128)(2,1)} fusion(s32[1280]{0:T(1024)S(1)} %fusion.80, bf16[128,2048]{1,0:T(8,128)(2,1)S(1)} %fusion.61, s32[2048]{0:T(1024)S(1)} %pad_clamp_fusion.1, bf16[]{:T(256)} %constant.105.clone.1), kind=kCustom, calls=%fused_computation.26 | custom fusion | bytes 6291458 | tf_op jit(solution)/shard_map/scatter | solution.py:138
  46.1 11.0 %reshape.347 = bf16[128,2,6,2048]{3,2,1,0:T(8,128)(2,1)} reshape(bf16[1536,2048]{1,0:T(8,128)(2,1)} %scatter_custom_fusion) | data formatting | bytes 12582912 | tf_op jit(solution)/shard_map/reshape | solution.py:140
  57.1 9.6 copy.75
  66.7 110.7 %all_to_all.10 = bf16[128,2,6,2048]{3,1,2,0:T(2,128)(2,1)S(1)} all-to-all(bf16[128,2,6,2048]{3,1,2,0:T(2,128)(2,1)S(1)} %copy.75), channel_id=1, replica_groups=mesh['outer'=8,'inner'=16] {'outer','inner'}, dimensions={0} | all-to-all | bytes 12582912 | tf_op jit(solution)/shard_map/all_to_all | solution.py:142
  177.5 2.6 copy-done.9
  180.1 8.6 fusion.15
  188.7 19.6 %convert_bitcast_fusion = bf16[128,2,6,2048]{3,0,2,1:T(8,128)(2,1)} fusion(bf16[2,512,2048]{2,1,0:T(8,128)(2,1)} %param.26, f32[2,128,6,512]{3,1,2,0:T(8,128)} %fusion.15, bf16[2,2048,512]{2,1,0:T(8,128)(2,1)} %param.24, bf16[128,2,6,2048]{3,1,2,0:T(2,128)(2,1)} %copy-done.9), kind=kOutput, calls=%fused_computation.21 | convolution fusion | flops 6450315264 | bytes 24117248 | tf_op jit(solution)/shard_map/secf,efd->secd/dot_general | solution.py:82
  208.4 12.8 %copy.78 = bf16[128,2,6,2048]{3,1,2,0:T(2,128)(2,1)} copy(bf16[128,2,6,2048]{3,0,2,1:T(8,128)(2,1)} %convert_bitcast_fusion) | data formatting | bytes 12582912 | tf_op jit(solution)/shard_map/convert_element_type | solution.py:84
  221.1 7.9 all-to-all-start.1
  229.5 74.2 %all-to-all-done.1 = bf16[128,2,6,2048]{3,1,2,0:T(2,128)(2,1)} async-done(((bf16[128,2,6,2048]{3,1,2,0:T(2,128)(2,1)}), bf16[128,2,6,2048]{3,1,2,0:T(2,128)(2,1)}, u32[]{:S(2)}, u32[]{:S(2)}) %all-to-all-start.1) | async-done | bytes 6291488 | tf_op jit(solution)/shard_map/all_to_all | solution.py:147
  303.7 10.4 %copy.79 = bf16[128,2,6,2048]{3,2,1,0:T(8,128)(2,1)} copy(bf16[128,2,6,2048]{3,1,2,0:T(2,128)(2,1)} %all-to-all-done.1) | data formatting | bytes 12582912 | tf_op jit(solution)/shard_map/all_to_all | solution.py:147
  314.1 11.4 %reshape.348 = bf16[1536,2048]{1,0:T(8,128)(2,1)} reshape(bf16[128,2,6,2048]{3,2,1,0:T(8,128)(2,1)} %copy.79) | data formatting | bytes 12582912 | tf_op jit(solution)/shard_map/reshape | solution.py:149
  325.5 14.4 %gather_fusion = bf16[1280,2048]{1,0:T(8,128)(2,1)} fusion(bf16[1536,2048]{1,0:T(8,128)(2,1)} %reshape.348, s32[2048]{0:T(1024)S(1)} %pad_clamp_fusion), kind=kCustom, calls=%fused_computation.1 | custom fusion | bytes 10490880 | tf_op jit(solution)/shard_map/gather | solution.py:149
  339.9 10.3 %reshape.358 = f32[128,10,2048]{2,1,0:T(8,128)} reshape(bf16[1280,2048]{1,0:T(8,128)(2,1)} %gather_fusion) | data formatting | bytes 15728640 | tf_op jit(solution)/shard_map/convert_element_type | solution.py:149
  350.3 9.5 multiply_reduce_fusion
  361.0 8.2 convolution_convert_fusion
  369.3 4.0 collective-permute-start
  373.4 4.5 collective-permute-done
  382.2 3.4 fusion.50
  385.6 157.9 %custom-call.5 = f32[16,1,128,128]{2,3,1,0:T(8,128)S(1)} custom-call(f32[16,1,128,128]{3,2,1,0:T(8,128)} %fusion.50), custom_call_target="InvertDiagBlocksLowerTriangular" | custom-call | tf_op jit(solution)/shard_map/triangular_solve/custom-call.1 | solution.py:203
  550.3 3.0 fusion.89
  553.8 3.1 fusion.65
  556.9 2.8 fusion.88
  559.7 60.0 %all-gather.19.cloned.1.call-done = bf16[256,128,128]{2,1,0:T(8,128)(2,1)} async-done(((bf16[16,128,128]{2,1,0:T(8,128)(2,1)}), bf16[256,128,128]{2,1,0:T(8,128)(2,1)}) %all-gather.19.cloned.1.call-update) | async-done | bytes 8388624 | tf_op jit(solution)/shard_map/all_gather | solution.py:17
  619.7 72.5 %all-gather.17.cloned.1.call-done = bf16[256,128,128]{2,1,0:T(8,128)(2,1)} async-done(((bf16[16,128,128]{2,1,0:T(8,128)(2,1)}), bf16[256,128,128]{2,1,0:T(8,128)(2,1)}) %all-gather.17.cloned.1.call-update) | async-done | bytes 8388624 | tf_op jit(solution)/shard_map/all_gather | solution.py:17
  693.6 2.4 fusion.55
  697.2 167.4 %all-gather.11.cloned.1.call-done = bf16[16,2,16,128,128]{4,3,2,1,0:T(8,128)(2,1)} async-done(((bf16[1,2,16,128,128]{4,3,2,1,0:T(8,128)(2,1)}), bf16[16,2,16,128,128]{4,3,2,1,0:T(8,128)(2,1)}) %all-gather.11.cloned.1.call-update) | async-done | bytes 16777232 | tf_op jit(solution)/shard_map/all_gather | solution.py:44
  864.6 9.3 reduce_sum.94
  878.5 3.3 convolution_multiply_fusion
  881.8 25.8 %all-gather.13.cloned.1.call-done = bf16[8,16,128,128]{3,2,1,0:T(8,128)(2,1)} async-done(((bf16[1,16,128,128]{3,2,1,0:T(8,128)(2,1)}), bf16[8,16,128,128]{3,2,1,0:T(8,128)(2,1)}) %all-gather.13.cloned.1.call-update) | async-done | bytes 4194320 | tf_op jit(solution)/shard_map/all_gather | solution.py:51
  907.6 33.7 %all-gather.15.cloned.1.call-done = bf16[8,16,128,128]{3,2,1,0:T(8,128)(2,1)} async-done(((bf16[1,16,128,128]{3,2,1,0:T(8,128)(2,1)}), bf16[8,16,128,128]{3,2,1,0:T(8,128)(2,1)}) %all-gather.15.cloned.1.call-update) | async-done | bytes 4194320 | tf_op jit(solution)/shard_map/all_gather | solution.py:51
  941.4 12.7 %while.27 = (s32[]{:T(128)}, bf16[16,128,128]{2,1,0:T(8,128)(2,1)S(1)}, s32[]{:T(128)}, bf16[8,16,128,128]{3,2,1,0:T(8,128)(2,1)}, bf16[8,16,128,128]{3,2,1,0:T(8,128)(2,1)}, /*index=5*/s32[]{:T(128)}, s32[]{:T(128)}) while((s32[]{:T(128)}, bf16[16,128,128]{2,1,0:T(8,128)(2,1)S(1)}, s32[]{:T(128)}, ...), condition=%wide.region_15.17_spmd.clone, body=%wide.region_14.16_spmd.clone.sunk | while | flops 68157440 | bytes 3672671 | solution.py:66
  (149 shorter events, 44.6 us)
Async XLA Ops:
  7.2 352.9 %copy-start = (bf16[2048,32]{0,1:T(8,128)(2,1)S(1)}, bf16[2048,32]{0,1:T(8,128)(2,1)}, u32[]{:S(2)}) copy-start(bf16[2048,32]{0,1:T(8,128)(2,1)} %param.29) | copy-start | bytes 393220
  7.2 353.8 %all-gather.9.cloned.1.call-start = ((), (), s32[]{:S(2)}) async-start(), calls=%async_computation.2 | async-start | bytes 17825792 | tf_op jit(solution)/shard_map/all_gather | solution.py:156
  9.6 1.6 copy-start.10
  9.6 1.8 copy-start.20
  66.7 113.4 %copy-start.23 = (bf16[2,2048,512]{2,1,0:T(8,128)(2,1)S(1)}, bf16[2,2048,512]{2,1,0:T(8,128)(2,1)}, u32[]{:S(2)}) copy-start(bf16[2,2048,512]{2,1,0:T(8,128)(2,1)} %param.25) | copy-start | bytes 12582916
  177.5 2.6 copy-start.9
  221.1 8.0 copy-start.19
  221.1 8.2 copy-start.24
  221.1 8.4 copy-start.17
  221.1 82.6 %all-to-all-start.1 = ((bf16[128,2,6,2048]{3,1,2,0:T(2,128)(2,1)}), bf16[128,2,6,2048]{3,1,2,0:T(2,128)(2,1)}, u32[]{:S(2)}, u32[]{:S(2)}) async-start(bf16[128,2,6,2048]{3,1,2,0:T(2,128)(2,1)} %copy.78), calls=%async_computation.1 | async-start | bytes 12582912 | tf_op jit(solution)/shard_map/all_to_all | solution.py:147
  229.1 390.6 %all-gather.19.cloned.1.call-start = ((), (), s32[]{:S(2)}) async-start(), calls=%async_computation.7 | async-start | bytes 8912896 | tf_op jit(solution)/shard_map/all_gather | solution.py:17
  350.2 9.8 %copy-start.18 = (f32[2048]{0:T(1024)S(1)}, f32[2048]{0:T(1024)}, u32[]{:S(2)}) copy-start(f32[2048]{0:T(1024)} %param.27) | copy-start | bytes 24580
  350.3 10.2 %copy-start.21 = (f32[16]{0:T(128)S(1)}, f32[16]{0:T(128)}, u32[]{:S(2)}) copy-start(f32[16]{0:T(128)} %param.32) | copy-start | bytes 196
  360.0 9.2 copy-start.16
  369.3 8.6 collective-permute-start
  379.5 1.7 copy-start.8
  381.2 162.4 %slice-start = ((f32[128,4096]{1,0:T(8,128)}), f32[128,2048]{1,0:T(8,128)S(1)}, s32[]{:S(2)}) async-start(f32[128,4096]{1,0:T(8,128)} %copy-done.8), calls=%async_computation.8 | async-start | bytes 2097152 | tf_op jit(solution)/shard_map/slice | solution.py:183
  543.6 6.7 copy-start.11
  548.6 1.7 copy-start.4
  550.3 3.5 copy-start.12
  553.3 138.8 %all-gather.17.cloned.1.call-start = ((), (), s32[]{:S(2)}) async-start(), calls=%async_computation.6 | async-start | bytes 8912896 | tf_op jit(solution)/shard_map/all_gather | solution.py:17
  556.9 135.3 %copy-start.6 = (f32[16,128,128]{2,1,0:T(8,128)}, f32[16,128,128]{2,1,0:T(8,128)S(1)}, u32[]{:S(2)}) copy-start(f32[16,128,128]{2,1,0:T(8,128)S(1)} %fusion.65) | copy-start | bytes 3145732
  559.6 305.0 %all-gather.11.cloned.1.call-start = ((), (), s32[]{:S(2)}) async-start(), calls=%async_computation.3 | async-start | bytes 17825792 | tf_op jit(solution)/shard_map/all_gather | solution.py:44
  697.1 210.5 %all-gather.13.cloned.1.call-start = ((), (), s32[]{:S(2)}) async-start(), calls=%async_computation.4 | async-start | bytes 4718592 | tf_op jit(solution)/shard_map/all_gather | solution.py:51
  875.0 66.4 %all-gather.15.cloned.1.call-start = ((), (), s32[]{:S(2)}) async-start(), calls=%async_computation.5 | async-start | bytes 4718592 | tf_op jit(solution)/shard_map/all_gather | solution.py:51
  875.6 3.0 copy-start.14
  954.0 1.2 copy-start.5
  954.0 1.5 copy-start.7
  954.1 2.7 copy-start.3
  955.6 3.1 copy-start.15
  956.8 3.9 copy-start.22
  956.8 5.1 copy-start.1
  (2 other events, 2.0 us)
Sparse Core Ops, SparseCore 0:
  10.1 187.0 all-gather.8
  553.5 66.1 all-gather.18
  621.8 70.3 all-gather.16
  697.2 167.3 all-gather.10
  875.1 32.4 all-gather.12
  909.2 32.1 all-gather.14
